TPU v7x, 256 devices: a whole 4x4x8 slice. The times are simulated.
256 devices in a mesh: sec: 32 (over z, x), op: 8 (over y, core).
Axes of the slice: x: 4, y: 4, z: 8, core: 2. Of those that a mesh axis runs over, the one named last changes fastest.
Arguments:
- wavefunction: bfloat16 [64, 512, 512], P('sec'), may hold values from -24 to 24
- left_blocks: bfloat16 [32, 64, 512, 512], P('op', 'sec'), may hold values from -5 to 5
- right_blocks: bfloat16 [32, 512, 512], P('op'), may hold values from -1 to 1
- charge_shifts: int32 [32], P('op'), may hold values from -2 to 2, as said below
- sector_rows: int32 [64], replicated, may hold values from 64 to 512, as said below
Outputs:
- next_vector: bfloat16 [64, 512, 512], P('sec')
- lanczos_coefficients: float32 [2, 3], replicated
Inputs may be any that keep to these rules, and one draw needn't show every extreme that they name: `charge_shifts`: some term has offset 2, some has offset -2, and some has offset 0. `sector_rows`: multiples of 64; some sector has 512 rows.
All inputs are finite; a program needn't handle non-finite values.
Results may differ from a plain program's by a relative error of at most 0.025.
Values may be sent and summed in bfloat16 or wider, within the bound.
A program may use at most 64 MiB of HBM per device.

v0:
```python
import jax
import jax.numpy as jnp
from jax import lax
from jax.sharding import PartitionSpec as P

PRODUCTS = 3


def extended(shard, sides, width):
    for axis, dim in sides:
        size, length = (lax.axis_size(axis), shard.shape[dim])
        up = [(i, (i + 1) % size) for i in range(size - 1)]
        down = [(j, i) for i, j in up]
        last = lax.slice_in_dim(shard, length - width, length, axis=dim)
        initial = lax.slice_in_dim(shard, 0, width, axis=dim)
        before = lax.ppermute(last, axis, up)
        after = lax.ppermute(initial, axis, down)
        shard = jnp.concatenate([before, shard, after], axis=dim)
    return shard


def on_device(wavefunction, left_blocks, right_blocks, charge_shifts, sector_rows):
    sectors_here, block_rows, right_width = wavefunction.shape
    terms_here = left_blocks.shape[0]
    first_sector = lax.axis_index("sec") * sectors_here
    local_rows = lax.dynamic_slice_in_dim(sector_rows, first_sector, sectors_here, 0)
    positions = jnp.arange(block_rows, dtype=jnp.int32)
    row_mask = (positions[None, :] < local_rows[:, None]).astype(jnp.float32)[:, :, None]
    live_count = right_width * jnp.sum(sector_rows).astype(jnp.float32)
    masked_start = wavefunction.astype(jnp.float32) * row_mask
    start_total = lax.psum(jnp.sum(masked_start * masked_start), "sec")
    vector = (masked_start / jnp.sqrt(start_total / live_count)).astype(jnp.bfloat16)
    alphas = []
    betas = []
    previous = jnp.zeros((sectors_here, block_rows, right_width), jnp.float32)
    beta = jnp.float32(0.0)
    for product in range(PRODUCTS):
        padded = extended(vector, (("sec", 0),), sectors_here)
        partial_value = jnp.zeros((sectors_here, block_rows, right_width), jnp.float32)
        for term in range(terms_here):
            window = lax.dynamic_slice_in_dim(
                padded, sectors_here - charge_shifts[term], sectors_here, 0
            )
            right_part = jnp.einsum(
                "sbn,nm->sbm", window, right_blocks[term], preferred_element_type=jnp.float32
            ).astype(jnp.bfloat16)
            partial_value = partial_value + jnp.einsum(
                "sab,sbm->sam", left_blocks[term], right_part, preferred_element_type=jnp.float32
            )
        image = lax.psum(partial_value.astype(jnp.bfloat16), "op").astype(jnp.float32) * row_mask
        current = vector.astype(jnp.float32)
        alpha = lax.psum(jnp.sum(current * image), "sec") / live_count
        residual = image - alpha * current - beta * previous
        beta = jnp.sqrt(lax.psum(jnp.sum(residual * residual), "sec") / live_count)
        previous = current
        vector = (residual / beta).astype(jnp.bfloat16)
        alphas.append(alpha)
        betas.append(beta)
    return (vector, jnp.stack([jnp.stack(alphas), jnp.stack(betas)]))


def solution(mesh):
    in_specs = (P("sec", None, None), P("op", "sec", None, None), P("op", None, None), P("op"), P())
    out_specs = (P("sec", None, None), P())
    return jax.shard_map(
        on_device, mesh=mesh, in_specs=in_specs, out_specs=out_specs, check_vma=False
    )
```

profile of v0, /device:TPU:2, one launch (start us, length us, event | category | flops | bytes accessed | tf_op | source)
XLA Modules:
  0.0 877.0 jit_solution(4391738130055484930)
XLA Ops:
  12.6 74.4 %psum.70 = f32[]{:T(128)} all-reduce(f32[]{:T(128)} %multiply_reduce_fusion.3), channel_id=1, replica_groups=mesh['sec'=32,'op'=8] {'sec'}, use_global_device_ids=true, to_apply=%region_1.0 | all-reduce | flops 1 | bytes 8 | tf_op jit(solution)/shard_map/psum | solution.py:31
  87.9 6.4 collective-permute-start.1
  102.0 4.6 collective-permute-done.1
  106.6 4.5 collective-permute-done
  117.0 4.4 fusion.12
  121.3 4.4 fusion.11
  125.7 5.3 fusion.8
  131.1 65.6 %all-reduce.4.cloned.1.call-done = bf16[2,512,512]{1,2,0:T(8,128)(2,1)} async-done(((bf16[2,512,512]{1,2,0:T(8,128)(2,1)}), bf16[2,512,512]{1,2,0:T(8,128)(2,1)}) %all-reduce.4.cloned.1.call-update) | async-done | bytes 1048592 | tf_op jit(solution)/shard_map/psum | solution.py:50
  199.1 71.8 %psum.72 = f32[]{:T(128)} all-reduce(f32[]{:T(128)} %fusion.3), channel_id=1, replica_groups=mesh['sec'=32,'op'=8] {'sec'}, use_global_device_ids=true, to_apply=%region_5.0 | all-reduce | flops 1 | bytes 8 | tf_op jit(solution)/shard_map/psum | solution.py:52
  272.8 74.7 %psum.73 = f32[]{:T(128)} all-reduce(f32[]{:T(128)} %multiply_reduce_fusion.2), channel_id=1, replica_groups=mesh['sec'=32,'op'=8] {'sec'}, use_global_device_ids=true, to_apply=%region_7.0 | all-reduce | flops 1 | bytes 8 | tf_op jit(solution)/shard_map/psum | solution.py:54
  354.8 10.7 %collective-permute-done.3 = bf16[2,512,512]{1,2,0:T(8,128)(2,1)S(1)} collective-permute-done((bf16[2,512,512]{1,2,0:T(8,128)(2,1)S(1)}, bf16[2,512,512]{1,2,0:T(8,128)(2,1)S(1)}, u32[]{:S(2)}, u32[]{:S(2)}) %collective-permute-start.3) | collective-permute-done | bytes 1048608 | tf_op jit(solution)/shard_map/ppermute | solution.py:17
  369.2 4.4 fusion.16
  373.6 4.4 fusion.15
  382.3 5.9 fusion.9
  388.3 66.4 %all-reduce.6.cloned.1.call-done = bf16[2,512,512]{1,2,0:T(8,128)(2,1)} async-done(((bf16[2,512,512]{1,2,0:T(8,128)(2,1)}), bf16[2,512,512]{1,2,0:T(8,128)(2,1)}) %all-reduce.6.cloned.1.call-update) | async-done | bytes 1048592 | tf_op jit(solution)/shard_map/psum | solution.py:50
  457.1 71.7 %psum.75 = f32[]{:T(128)} all-reduce(f32[]{:T(128)} %fusion.6), channel_id=1, replica_groups=mesh['sec'=32,'op'=8] {'sec'}, use_global_device_ids=true, to_apply=%region_10.0 | all-reduce | flops 1 | bytes 8 | tf_op jit(solution)/shard_map/psum | solution.py:52
  530.9 74.7 %psum.76 = f32[]{:T(128)} all-reduce(f32[]{:T(128)} %multiply_reduce_fusion.1), channel_id=1, replica_groups=mesh['sec'=32,'op'=8] {'sec'}, use_global_device_ids=true, to_apply=%region_12.0 | all-reduce | flops 1 | bytes 8 | tf_op jit(solution)/shard_map/psum | solution.py:54
  614.2 10.8 %collective-permute-done.5 = bf16[2,512,512]{1,2,0:T(8,128)(2,1)S(1)} collective-permute-done((bf16[2,512,512]{1,2,0:T(8,128)(2,1)S(1)}, bf16[2,512,512]{1,2,0:T(8,128)(2,1)S(1)}, u32[]{:S(2)}, u32[]{:S(2)}) %collective-permute-start.5) | collective-permute-done | bytes 1048608 | tf_op jit(solution)/shard_map/ppermute | solution.py:17
  628.8 4.4 fusion.19
  633.2 4.4 fusion.18
  641.9 5.9 fusion.10
  647.9 66.4 %all-reduce.8.cloned.1.call-done = bf16[2,512,512]{1,2,0:T(8,128)(2,1)} async-done(((bf16[2,512,512]{1,2,0:T(8,128)(2,1)}), bf16[2,512,512]{1,2,0:T(8,128)(2,1)}) %all-reduce.8.cloned.1.call-update) | async-done | bytes 1048592 | tf_op jit(solution)/shard_map/psum | solution.py:50
  716.7 71.7 %psum.78 = f32[]{:T(128)} all-reduce(f32[]{:T(128)} %fusion), channel_id=1, replica_groups=mesh['sec'=32,'op'=8] {'sec'}, use_global_device_ids=true, to_apply=%region_15.0 | all-reduce | flops 1 | bytes 8 | tf_op jit(solution)/shard_map/psum | solution.py:52
  790.4 74.7 %psum.79 = f32[]{:T(128)} all-reduce(f32[]{:T(128)} %multiply_reduce_fusion), channel_id=1, replica_groups=mesh['sec'=32,'op'=8] {'sec'}, use_global_device_ids=true, to_apply=%region_17.0 | all-reduce | flops 1 | bytes 8 | tf_op jit(solution)/shard_map/psum | solution.py:54
  (47 shorter events, 60.1 us)
Async XLA Ops:
  7.2 189.5 %all-reduce.4.cloned.1.call-start = ((), (), s32[]{:S(2)}) async-start(), calls=%async_computation | async-start | bytes 2097152 | tf_op jit(solution)/shard_map/psum | solution.py:50
  10.8 85.4 %copy-start.3 = (s32[4]{0:T(128)S(1)}, s32[4]{0:T(128)}, u32[]{:S(2)}) copy-start(s32[4]{0:T(128)} %param.8) | copy-start | bytes 52
  87.9 18.7 %collective-permute-start.1 = (bf16[2,512,512]{1,2,0:T(8,128)(2,1)S(1)}, bf16[2,512,512]{1,2,0:T(8,128)(2,1)S(1)}, u32[]{:S(2)}, u32[]{:S(2)}) collective-permute-start(bf16[2,512,512]{1,2,0:T(8,128)(2,1)S(1)} %divide_convert_fusion.3), channel_id=1, source_target_pairs={{8,0},{16,8},{24,16},{32,24},{40,32},{48,40},{56,48},{64,56},{72,6... | collective-permute-start | bytes 3145736 | tf_op jit(solution)/shard_map/ppermute | solution.py:17
  94.3 16.8 %collective-permute-start = (bf16[2,512,512]{1,2,0:T(8,128)(2,1)S(1)}, bf16[2,512,512]{1,2,0:T(8,128)(2,1)}, u32[]{:S(2)}, u32[]{:S(2)}) collective-permute-start(bf16[2,512,512]{1,2,0:T(8,128)(2,1)S(1)} %divide_convert_fusion.3), channel_id=1, source_target_pairs={{0,8},{8,16},{16,24},{24,32},{32,40},{40,48},{48,56},{56,64},{64,7... | collective-permute-start | bytes 3145736 | tf_op jit(solution)/shard_map/ppermute | solution.py:16
  131.1 323.6 %all-reduce.6.cloned.1.call-start = ((), (), s32[]{:S(2)}) async-start(), calls=%async_computation.1 | async-start | bytes 2097152 | tf_op jit(solution)/shard_map/psum | solution.py:50
  196.7 74.9 %copy-start.2 = (bf16[2,512,512]{1,2,0:T(8,128)(2,1)S(1)}, bf16[2,512,512]{1,2,0:T(8,128)(2,1)}, u32[]{:S(2)}) copy-start(bf16[2,512,512]{1,2,0:T(8,128)(2,1)} %all-reduce.4.cloned.1.call-done) | copy-start | bytes 3145732
  348.7 16.7 %collective-permute-start.3 = (bf16[2,512,512]{1,2,0:T(8,128)(2,1)S(1)}, bf16[2,512,512]{1,2,0:T(8,128)(2,1)S(1)}, u32[]{:S(2)}, u32[]{:S(2)}) collective-permute-start(bf16[2,512,512]{1,2,0:T(8,128)(2,1)S(1)} %divide_convert_fusion.2), channel_id=1, source_target_pairs={{8,0},{16,8},{24,16},{32,24},{40,32},{48,40},{56,48},{64,56},{72,6... | collective-permute-start | bytes 3145736 | tf_op jit(solution)/shard_map/ppermute | solution.py:17
  350.7 16.7 %collective-permute-start.2 = (bf16[2,512,512]{1,2,0:T(8,128)(2,1)S(1)}, bf16[2,512,512]{1,2,0:T(8,128)(2,1)S(1)}, u32[]{:S(2)}, u32[]{:S(2)}) collective-permute-start(bf16[2,512,512]{1,2,0:T(8,128)(2,1)S(1)} %divide_convert_fusion.2), channel_id=1, source_target_pairs={{0,8},{8,16},{16,24},{24,32},{32,40},{40,48},{48,56},{56,64},{64,7... | collective-permute-start | bytes 3145736 | tf_op jit(solution)/shard_map/ppermute | solution.py:16
  388.2 326.0 %all-reduce.8.cloned.1.call-start = ((), (), s32[]{:S(2)}) async-start(), calls=%async_computation.2 | async-start | bytes 2097152 | tf_op jit(solution)/shard_map/psum | solution.py:50
  454.6 74.9 %copy-start = (bf16[2,512,512]{1,2,0:T(8,128)(2,1)S(1)}, bf16[2,512,512]{1,2,0:T(8,128)(2,1)}, u32[]{:S(2)}) copy-start(bf16[2,512,512]{1,2,0:T(8,128)(2,1)} %all-reduce.6.cloned.1.call-done) | copy-start | bytes 3145732
  608.4 16.7 %collective-permute-start.5 = (bf16[2,512,512]{1,2,0:T(8,128)(2,1)S(1)}, bf16[2,512,512]{1,2,0:T(8,128)(2,1)S(1)}, u32[]{:S(2)}, u32[]{:S(2)}) collective-permute-start(bf16[2,512,512]{1,2,0:T(8,128)(2,1)S(1)} %divide_convert_fusion.1), channel_id=1, source_target_pairs={{8,0},{16,8},{24,16},{32,24},{40,32},{48,40},{56,48},{64,56},{72,6... | collective-permute-start | bytes 3145736 | tf_op jit(solution)/shard_map/ppermute | solution.py:17
  610.3 16.7 %collective-permute-start.4 = (bf16[2,512,512]{1,2,0:T(8,128)(2,1)S(1)}, bf16[2,512,512]{1,2,0:T(8,128)(2,1)S(1)}, u32[]{:S(2)}, u32[]{:S(2)}) collective-permute-start(bf16[2,512,512]{1,2,0:T(8,128)(2,1)S(1)} %divide_convert_fusion.1), channel_id=1, source_target_pairs={{0,8},{8,16},{16,24},{24,32},{32,40},{40,48},{48,56},{56,64},{64,7... | collective-permute-start | bytes 3145736 | tf_op jit(solution)/shard_map/ppermute | solution.py:16
  714.3 74.9 %copy-start.1 = (bf16[2,512,512]{1,2,0:T(8,128)(2,1)S(1)}, bf16[2,512,512]{1,2,0:T(8,128)(2,1)}, u32[]{:S(2)}) copy-start(bf16[2,512,512]{1,2,0:T(8,128)(2,1)} %all-reduce.8.cloned.1.call-done) | copy-start | bytes 3145732
Sparse Core Ops, SparseCore 0:
  131.2 65.4 all-reduce.3
  388.4 66.2 all-reduce.5
  648.0 66.2 all-reduce.7
where the time goes:
time: 878 us; the launch traced here: 877 us
  blocking collectives  514 us (59%)
  waiting for transfers between devices  233 us (27%)
  matrix products  55.1 us (6%)
  other arithmetic  25.5 us (3%)
  between operations  24.4 us (3%)
  starting transfers between devices  20.3 us (2%)
    psum x3, blocking collectives, on_device(): beta = jnp.sqrt(lax.psum(jnp.sum(residual * residual), 'sec') / live_count)  224 us
    psum x3, blocking collectives, on_device(): alpha = lax.psum(jnp.sum(current * image), 'sec') / live_count  215 us
    psum x3, waiting for transfers between devices, on_device(): lax.psum(partial_value.astype(jnp.bfloat16), 'op').astype(jnp.float32)  198 us
    psum x1, blocking collectives, on_device(): start_total = lax.psum(jnp.sum(masked_start * masked_start), 'sec')  74.4 us
    dot_general x12, matrix products, on_device(): jnp.einsum('sab,sbm->sam', left_blocks[term], right_part, preferred_eleme...  55.1 us
    ppermute x3, waiting for transfers between devices, extended(): after = lax.ppermute(initial, axis, down)  26.1 us
  transfers between devices with their start and end apart: 9, of which 9 were waited for; matrix products, arithmetic and copies ran while one was open for 0% of the time, Pallas kernels for 0%

commit v1 on v0

v1 whole, which is shorter than its diff:
```python
import functools

import jax
import jax.numpy as jnp
from jax import lax
from jax.experimental import pallas as pl
from jax.experimental.pallas import tpu as pltpu
from jax.sharding import PartitionSpec as P

MESH = pl.DeviceIdType.MESH
PRODUCTS = 3
F32 = jnp.float32
BF16 = jnp.bfloat16
QUARTERS = 4
ZERO_SLOT = 6
X_CHIPS = 4


class Places:
    def __init__(self, sec_size, op_size):
        self.sec_size, self.op_size = sec_size, op_size
        self.sec = lax.axis_index("sec")
        self.op = lax.axis_index("op")
        self.y, self.core = self.op // 2, self.op % 2
        self.z, self.x = self.sec // X_CHIPS, self.sec % X_CHIPS
        self.y_size = op_size // 2
        self.z_size = sec_size // X_CHIPS

    def sibling(self):
        return (self.sec, self.y * 2 + (1 - self.core))

    def along_y(self, step):
        return (self.sec, ((self.y + step + self.y_size) % self.y_size) * 2 + self.core)

    def along_sec(self, step):
        return ((self.sec + step + self.sec_size) % self.sec_size, self.op)

    def op_peer(self, step):
        return (self.op + step) % self.op_size

    def x_peer(self, step):
        return (self.x + step) % X_CHIPS

    def z_peer(self, step):
        return (self.z + step) % self.z_size


def lanczos_kernel(
    sec_size, op_size, shift_ref, rows_ref, wave_hbm, left_hbm, right_hbm, out_ref, coef_ref, *scratch
):
    scratch = list(scratch)
    take = lambda count: [scratch.pop(0) for _ in range(count)]
    left, right, parts = take(3)
    vectors = [take(QUARTERS) for _ in range(PRODUCTS)] + [take(QUARTERS)]
    sib_out, sib_in, y_out, y_in = take(4)
    shard_v, shard_h, shard_own = take(3)
    op_tiles, x_tiles, z_tiles = (take(PRODUCTS + 1) for _ in range(3))
    own = [None] + take(PRODUCTS)
    load_sem, ext_sem, sib_sem, rs_sib_sem, rs_y_sem, send_sem, op_sem, x_sem, z_sem, tile_sem = take(10)
    block, width = parts.shape[0] // 8, parts.shape[1]
    quarter = block // QUARTERS
    half = quarter // 2
    at = Places(sec_size, op_size)
    core = at.core
    sent = [0] * (PRODUCTS + 1)

    def row_start(r):
        return pl.multiple_of(((at.y + r) % QUARTERS) * quarter, quarter)

    loads = []
    for r in range(QUARTERS):
        for n, sector in enumerate((core, 1 - core)):
            loads.append(
                pltpu.make_async_copy(
                    wave_hbm.at[sector, pl.ds(row_start(r), quarter), :],
                    vectors[0][r].at[n * 3],
                    load_sem.at[2 * r + n],
                )
            )
    loads.append(pltpu.make_async_copy(right_hbm, right, load_sem.at[8]))
    loads.append(pltpu.make_async_copy(left_hbm, left, load_sem.at[9]))
    for copy in loads:
        copy.start()

    for k in range(PRODUCTS):
        for r in range(QUARTERS):
            vectors[k][r][ZERO_SLOT] = jnp.zeros((quarter, width), BF16)
    for copy in loads[:8]:
        copy.wait()

    barrier = pltpu.get_barrier_semaphore()
    partners = [(at.sec, at.op_peer(s)) for s in range(1, op_size)]
    partners += [(at.z * X_CHIPS + at.x_peer(s), at.op) for s in range(1, X_CHIPS)]
    partners += [(at.z_peer(s) * X_CHIPS + at.x, at.op) for s in range(1, at.z_size)]
    partners += [at.along_sec(1), at.along_sec(-1)]
    for partner in partners:
        pl.semaphore_signal(barrier, inc=1, device_id=partner, device_id_type=MESH)

    live_rows = lax.fori_loop(0, rows_ref.shape[0], lambda i, total: total + rows_ref[i], jnp.int32(0))
    live = jnp.full((1, 1), live_rows * width, jnp.int32).astype(F32)
    my_rows = rows_ref[2 * at.sec + core]

    pl.semaphore_wait(barrier, len(partners))

    flying = []

    def remote(src, dst, to, recv, pool):
        return pltpu.make_async_remote_copy(
            src_ref=src, dst_ref=dst, send_sem=send_sem.at[pool, sent[pool]], recv_sem=recv, device_id=to,
            device_id_type=MESH,
        )

    def launch(copy, pool):
        copy.start()
        flying.append(copy)
        sent[pool] += 1

    def piece(k, r, j, h):
        return vectors[k][r].at[j, pl.ds(h * half, half), :]

    def slot(k, side, mine):
        return side + (0 if mine else 3 if k < PRODUCTS else 1)

    def send_piece(k, side, r, h, kind):
        src = piece(k, r, slot(k, side, True), h)
        if k > 0 and side == 0 and r == 0:
            src = own[k].at[pl.ds(h * half, half), :]
        if kind == "sib":
            to, r_to, side_to, sem = at.sibling(), r, side, sib_sem
        elif kind == "y+":
            to, r_to, side_to, sem = at.along_y(1), (r - 1) % QUARTERS, side, ext_sem
        elif kind == "y-":
            to, r_to, side_to, sem = at.along_y(-1), (r + 1) % QUARTERS, side, ext_sem
        elif kind == "x+":
            to, r_to, side_to, sem = at.along_sec(1), r, 1, ext_sem
        else:
            to, r_to, side_to, sem = at.along_sec(-1), r, 2, ext_sem
        dst = piece(k, r_to, slot(k, side_to, kind != "sib"), h)
        launch(remote(src, dst, to, sem.at[k, r_to, side_to, h], k), k)

    def wait_piece(k, side, r, h, sem, mine):
        here = piece(k, r, slot(k, side, mine), h)
        remote(here, here, at.sibling(), sem.at[k, r, side, h], k).wait_recv()

    def arrive(k, side, r, h, kinds):
        wait_piece(k, side, r, h, ext_sem, True)
        for kind in kinds:
            send_piece(k, side, r, h, kind)

    def right_products(k, r):
        first = row_start(r)
        ids = first + lax.broadcasted_iota(jnp.int32, (quarter, 1), 0)

        def body(term, carry):
            for target in range(2):
                shift = shift_ref[term]
                source = 2 * at.sec + target - shift
                valid = jnp.logical_and(source >= 0, source < 2 * sec_size)
                offset = target - shift
                side = jnp.where(offset < 0, 1, jnp.where(offset > 1, 2, 0))
                j = jnp.where((offset + 2) % 2 == core, side, side + 3)
                j = jnp.where(valid, j, ZERO_SLOT)
                value = jnp.dot(vectors[k][r][j], right[term], preferred_element_type=F32)
                if k == 0:
                    limit = rows_ref[jnp.clip(source, 0, 2 * sec_size - 1)]
                    value = jnp.where(ids < limit, value, 0.0)
                place = pl.multiple_of((term * 2 + target) * block + first, quarter)
                parts[pl.ds(place, quarter), :] = value.astype(BF16)
            return carry

        lax.fori_loop(0, 4, body, 0)

    def left_products(target, r):
        first = row_start(r)
        total = None
        for term in range(4):
            place = pl.multiple_of((term * 2 + target) * block, block)
            value = jnp.dot(
                left[term, target, pl.ds(first, quarter), :],
                parts[pl.ds(place, block), :],
                preferred_element_type=F32,
            )
            total = value if total is None else total + value
        return total

    def fold(value):
        folded = value[0:8]
        for i in range(8, value.shape[0], 8):
            folded = folded + value[i : i + 8]
        total = folded[:, 0:128]
        for i in range(128, width, 128):
            total = total + folded[:, i : i + 128]
        return total

    tile_count = [0] * (PRODUCTS + 1)

    def spread(tiles, sem, n, tile, count, partner):
        tiles[n][0] = tile
        for s in range(1, count):
            copy = pltpu.make_async_remote_copy(
                src_ref=tiles[n].at[0], dst_ref=tiles[n].at[count - s], send_sem=tile_sem.at[n, tile_count[n]],
                recv_sem=sem.at[n, count - s], device_id=partner(s), device_id_type=MESH,
            )
            copy.start()
            flying.append(copy)
            tile_count[n] += 1

    def gathered(tiles, sem, n, count, me):
        for s in range(1, count):
            pltpu.make_async_remote_copy(
                src_ref=tiles[n].at[s], dst_ref=tiles[n].at[s], send_sem=tile_sem.at[n, 0],
                recv_sem=sem.at[n, s], device_id=at.sibling(), device_id_type=MESH,
            ).wait_recv()
        total = None
        for i in range(count):
            tile = tiles[n][(i + count - me) % count]
            total = tile if total is None else total + tile
        return total

    def reduce_op(n, sums):
        tile = jnp.concatenate([jnp.sum(s, axis=0, keepdims=True) for s in sums], axis=0)
        tile = jnp.concatenate([tile, jnp.zeros((8 - len(sums), 128), F32)], axis=0)
        spread(op_tiles, op_sem, n, tile, op_size, lambda s: (at.sec, at.op_peer(s)))

    def reduce_x(n):
        tile = gathered(op_tiles, op_sem, n, op_size, at.op)
        spread(x_tiles, x_sem, n, tile, X_CHIPS, lambda s: (at.z * X_CHIPS + at.x_peer(s), at.op))

    def reduce_z(n):
        tile = gathered(x_tiles, x_sem, n, X_CHIPS, at.x)
        spread(z_tiles, z_sem, n, tile, at.z_size, lambda s: (at.z_peer(s) * X_CHIPS + at.x, at.op))

    def reduced(n):
        sums = jnp.sum(gathered(z_tiles, z_sem, n, at.z_size, at.z), axis=1, keepdims=True)
        return [sums[q : q + 1] / live for q in range(4)]

    step_rows = 32 if quarter % 32 == 0 else 16
    zero_sum = jnp.zeros((8, 128), F32)

    def blocks(body, carry):
        for first in range(0, quarter, step_rows):
            rows = pl.ds(first, step_rows)
            ids = at.y * quarter + first + lax.broadcasted_iota(jnp.int32, (step_rows, 1), 0)
            carry = body(rows, ids < my_rows, carry)
        return carry

    halo_y = {0: lambda r, h: r in (1, 3), 1: lambda r, h: r in (1, 3) and h == 1}
    via_y = lambda k, r, h: halo_y[min(k, 1)](r, h)

    for h in range(2):
        for kind in ("x+", "x-"):
            send_piece(0, 0, 0, h, kind)
    for h in range(2):
        for kind in ("x+", "x-"):
            send_piece(0, 0, 2, h, kind)

    def start_sum(rows, alive, carry):
        value = jnp.where(alive, vectors[0][0][0, rows, :].astype(F32), 0.0)
        return carry + fold(value * value)

    norm = blocks(start_sum, zero_sum)
    reduce_op(0, [norm, zero_sum, zero_sum, zero_sum])

    def halo_first(k):
        for h in range(2):
            for side in (1, 2):
                kinds = ["y+", "y-"] if via_y(k, 1, h) else []
                arrive(k, side, 0, h, kinds + ["sib"])

    def halo_rest(k, rs):
        for h in range(2):
            for r in rs:
                for side in (1, 2):
                    arrive(k, side, r, h, ["sib"])

    def from_sibling(k, sides, r):
        for side in sides:
            for h in range(2):
                wait_piece(k, side, r, h, sib_sem, False)

    alphas, betas = [], []
    shift_a = scale_b = guess = None
    combos = []
    for k in range(PRODUCTS):
        sides = (1, 2) if k == 0 else (0, 1, 2)
        if k > 0:
            for h in range(2):
                arrive(k, 0, 3, h, (["y+"] if h == 0 else []) + ([] if via_y(k, 3, h) else ["x+", "x-"]) + ["sib"])
                arrive(k, 0, 1, h, (["y-"] if h == 1 else []) + ([] if via_y(k, 1, h) else ["x+", "x-"]) + ["sib"])
        halo_first(k)
        if k > 0:
            for h in range(2):
                arrive(k, 0, 2, h, ["x+", "x-", "sib"])
        reduce_x(k)
        from_sibling(k, sides, 0)
        if k > 0:
            kept.wait()
        if k == 0:
            loads[8].wait()
        right_products(k, 0)
        halo_rest(k, (1, 3))
        reduce_z(k)
        from_sibling(k, sides, 1)
        right_products(k, 1)
        from_sibling(k, sides, 3)
        right_products(k, 3)
        halo_rest(k, (2,))
        from_sibling(k, sides, 2)
        right_products(k, 2)
        if k == 0:
            loads[9].wait()

        for r in (2, 1, 3, 0):
            sib_out[k, r] = left_products(1 - core, r).astype(BF16)
            launch(remote(sib_out.at[k, r], sib_in.at[k, r], at.sibling(), rs_sib_sem.at[k, r], k), k)
        for r in (2, 1, 3, 0):
            value = left_products(core, r)
            remote(sib_in.at[k, r], sib_in.at[k, r], at.sibling(), rs_sib_sem.at[k, r], k).wait_recv()
            value = value + sib_in[k, r].astype(F32)
            if r == 0:
                shard_own[...] = value
            else:
                y_out[k, r - 1] = value.astype(BF16)
                launch(
                    remote(y_out.at[k, r - 1], y_in.at[k, 3 - r], at.along_y(r), rs_y_sem.at[k, 3 - r], k), k
                )

        s = reduced(k)
        if k == 0:
            a, b = jnp.zeros((1, 1), F32), jnp.sqrt(s[0])
            guess = jnp.zeros((1, 1), F32)
            next_guess = guess
        else:
            alpha = s[0]
            a = alpha - guess
            b = jnp.sqrt(s[1] - 2.0 * a * s[2] + a * a * s[3])
            alphas.append(alpha)
            betas.append(b)
            next_guess = alpha
        inv_b = 1.0 / b
        combos.append((a, inv_b))
        beta = betas[-1] if k > 0 else jnp.zeros((1, 1), F32)
        guess = next_guess

        for i in range(3):
            remote(y_in.at[k, i], y_in.at[k, i], at.sibling(), rs_y_sem.at[k, i], k).wait_recv()


        def shard_step(rows, alive, carry):
            product = shard_own[rows, :]
            for i in range(3):
                product = product + y_in[k, i, rows, :].astype(F32)
            product = jnp.where(alive, product, 0.0)
            u = (vectors[0][0][0, rows, :] if k == 0 else own[k][rows, :]).astype(F32)
            if k == 0:
                v = jnp.where(alive, u, 0.0) * inv_b
                image = product * inv_b
                new = image
            else:
                v_before = shard_v[(k - 1) % 2, rows, :]
                v = (u - a * v_before) * inv_b
                image = (product - a * shard_h[rows, :]) * inv_b
                new = image - guess * v - beta * v_before
            shard_v[k % 2, rows, :] = v
            shard_h[rows, :] = image
            new = new.astype(BF16)
            own[k + 1][rows, :] = new
            new = new.astype(F32)
            pairs = ((v, image), (new, new), (new, v), (v, v))
            return tuple(c + fold(p * q) for c, (p, q) in zip(carry, pairs))

        sums = blocks(shard_step, (zero_sum,) * 4)
        kinds = ("y+", "y-", "x+", "x-", "sib") if k + 1 < PRODUCTS else ("y+", "y-", "sib")
        for h in range(2):
            for kind in kinds:
                send_piece(k + 1, 0, 0, h, kind)
        kept = pltpu.make_async_copy(own[k + 1], vectors[k + 1][0].at[0], load_sem.at[10 + k])
        kept.start()
        reduce_op(k + 1, sums)

    n = PRODUCTS
    for h in range(2):
        arrive(n, 0, 3, h, (["y+"] if h == 0 else []) + ["sib"])
        arrive(n, 0, 1, h, (["y-"] if h == 1 else []) + ["sib"])
    reduce_x(n)
    for h in range(2):
        arrive(n, 0, 2, h, ["sib"])
    reduce_z(n)
    for r in range(QUARTERS):
        from_sibling(n, (0,), r)
    kept.wait()
    s = reduced(n)
    a = s[0] - guess
    b = jnp.sqrt(s[1] - 2.0 * a * s[2] + a * a * s[3])
    alphas.append(s[0])
    betas.append(b)
    combos.append((a, 1.0 / b))

    weights = [None] * 4
    factor = combos[3][1]
    weights[3] = factor
    for i in (2, 1, 0):
        factor = -factor * combos[i + 1][0] * combos[i][1]
        weights[i] = factor
    for r in range(QUARTERS):
        first = row_start(r)
        for n, t in enumerate((core, 1 - core)):
            limit = rows_ref[2 * at.sec + t]

            def final(i, carry, r=r, n=n, t=t, limit=limit, first=first):
                rows = pl.ds(pl.multiple_of(i * step_rows, step_rows), step_rows)
                ids = first + i * step_rows + lax.broadcasted_iota(jnp.int32, (step_rows, 1), 0)
                value = jnp.where(ids < limit, vectors[0][r][3 * n, rows, :].astype(F32), 0.0) * weights[0]
                for m in (1, 2):
                    value = value + vectors[m][r][3 * n, rows, :].astype(F32) * weights[m]
                value = value + vectors[3][r][n, rows, :].astype(F32) * weights[3]
                out_ref[t, pl.ds(pl.multiple_of(first + i * step_rows, step_rows), step_rows), :] = value.astype(BF16)
                return carry

            lax.fori_loop(0, quarter // step_rows, final, 0)

    row = lax.broadcasted_iota(jnp.int32, (8, 128), 0)
    lane = lax.broadcasted_iota(jnp.int32, (8, 128), 1)
    coefs = jnp.zeros((8, 128), F32)
    for i in range(PRODUCTS):
        coefs = jnp.where((row == 0) & (lane == i), alphas[i], coefs)
        coefs = jnp.where((row == 1) & (lane == i), betas[i], coefs)
    coef_ref[...] = coefs

    for copy in flying:
        copy.wait_send()


def on_device(sec_size, op_size, wavefunction, left_blocks, right_blocks, charge_shifts, sector_rows):
    sectors_here, block, width = wavefunction.shape
    terms = left_blocks.shape[0]
    quarter = block // QUARTERS
    z_size = sec_size // X_CHIPS
    dma = pltpu.SemaphoreType.DMA
    scratch = [
        pltpu.VMEM(left_blocks.shape, BF16),
        pltpu.VMEM(right_blocks.shape, BF16),
        pltpu.VMEM((terms * sectors_here * block, width), BF16),
    ]
    scratch += [pltpu.VMEM((ZERO_SLOT + 1, quarter, width), BF16) for _ in range(PRODUCTS * QUARTERS)]
    scratch += [pltpu.VMEM((sectors_here, quarter, width), BF16) for _ in range(QUARTERS)]
    scratch += [pltpu.VMEM((PRODUCTS, QUARTERS, quarter, width), BF16)] * 2
    scratch += [pltpu.VMEM((PRODUCTS, 3, quarter, width), BF16)] * 2
    scratch += [
        pltpu.VMEM((2, quarter, width), F32),
        pltpu.VMEM((quarter, width), F32),
        pltpu.VMEM((quarter, width), F32),
    ]
    rounds = PRODUCTS + 1
    scratch += [pltpu.VMEM((count, 8, 128), F32) for count in (op_size, X_CHIPS, z_size) for _ in range(rounds)]
    scratch += [pltpu.VMEM((quarter, width), BF16) for _ in range(PRODUCTS)]
    scratch += [
        dma((10 + PRODUCTS,)),
        dma((rounds, QUARTERS, 3, 2)),
        dma((rounds, QUARTERS, 3, 2)),
        dma((PRODUCTS, QUARTERS)),
        dma((PRODUCTS, 3)),
        dma((rounds, 64)),
        dma((rounds, op_size)),
        dma((rounds, X_CHIPS)),
        dma((rounds, z_size)),
        dma((rounds, op_size + X_CHIPS + z_size)),
    ]
    smem = pl.BlockSpec(memory_space=pltpu.SMEM)
    hbm = pl.BlockSpec(memory_space=pl.ANY)
    vmem = pl.BlockSpec(memory_space=pltpu.VMEM)
    vector, coefs = pl.pallas_call(
        functools.partial(lanczos_kernel, sec_size, op_size),
        out_shape=(
            jax.ShapeDtypeStruct(wavefunction.shape, BF16),
            jax.ShapeDtypeStruct((8, 128), F32),
        ),
        in_specs=[smem, smem, hbm, hbm, hbm],
        out_specs=(vmem, vmem),
        scratch_shapes=scratch,
        compiler_params=pltpu.CompilerParams(
            collective_id=0, has_side_effects=True, vmem_limit_bytes=56 * 1024 * 1024
        ),
    )(charge_shifts, sector_rows, wavefunction, left_blocks, right_blocks)
    return vector, coefs[0:2, 0:PRODUCTS]


def solution(mesh):
    in_specs = (P("sec", None, None), P("op", "sec", None, None), P("op", None, None), P("op"), P())
    out_specs = (P("sec", None, None), P())
    return jax.shard_map(
        functools.partial(on_device, mesh.shape["sec"], mesh.shape["op"]),
        mesh=mesh, in_specs=in_specs, out_specs=out_specs, check_vma=False,
    )
```

time: 878 us -> 123 us (0.14)
  blocking collectives: 514 us -> 0 us
  waiting for transfers between devices: 233 us -> 0 us
  Pallas kernels: 0 us -> 119 us
  matrix products: 55.1 us -> 0 us
  other arithmetic: 25.5 us -> 0 us
  between operations: 24.4 us -> 0.64 us
  starting transfers between devices: 20.3 us -> 0 us
    psum x7 -> x0, blocking collectives: 514 us -> none  [the longest x3 224 us: on_device(): beta = jnp.sqrt(lax.psum(jnp.sum(residual * residual), 'sec') / live_count)]
    psum x3 -> x0, waiting for transfers between devices: 198 us -> none  [on_device(): lax.psum(partial_value.astype(jnp.bfloat16), 'op').astype(jnp.float32)]
    pallas_call x0 -> x1, Pallas kernels: none -> 119 us  [on_device(): pl.pallas_call(functools.partial(lanczos_kernel, sec_size, op_size), out_...]
    dot_general x12 -> x0, matrix products: 55.1 us -> none  [on_device(): jnp.einsum('sab,sbm->sam', left_blocks[term], right_part, preferred_eleme...]
    ppermute x6 -> x0, waiting for transfers between devices: 34.5 us -> none  [the longest x3 26.1 us: extended(): after = lax.ppermute(initial, axis, down)]
    ppermute x6 -> x0, starting transfers between devices: 20.2 us -> none  [the longest x3 10.2 us: extended(): after = lax.ppermute(initial, axis, down)]
    reduce_sum x8 -> x0, other arithmetic: 13.7 us -> none  [the longest x3 7.38 us: on_device(): alpha = lax.psum(jnp.sum(current * image), 'sec') / live_count]
  transfers between devices with their start and end apart: 9 -> 0, of which waited for: 9 -> 0; matrix products, arithmetic and copies ran while one was open for 0% -> 0% of each run, Pallas kernels for 0% -> 0%
where the time goes in v1:
time: 123 us
  Pallas kernels  119 us (97%)
  local copies, waits for them, and re-layouts  3.5 us (3%)
    pallas_call x1, Pallas kernels, on_device(): pl.pallas_call(functools.partial(lanczos_kernel, sec_size, op_size), out_...  119 us

profile of v1, /device:TPU:2, one launch (start us, length us, event | category | flops | bytes accessed | tf_op | source)
XLA Modules:
  0.0 122.9 jit_solution(13454817309723748057)
XLA Ops:
  0.6 118.7 %shard_map.68 = (bf16[2,512,512]{2,1,0:T(8,128)(2,1)}, f32[8,128]{1,0:T(8,128)}) custom-call(s32[4]{0:T(128)} %shift_ref.1, s32[64]{0:T(128)} %rows_ref.1, bf16[2,512,512]{2,1,0:T(8,128)(2,1)} %wave_hbm.1, bf16[4,2,512,512]{3,2,1,0:T(8,128)(2,1)} %left_hbm.1, bf16[4,512,512]{2,1,0:T(8,128)(2,1)} %right_hbm.1), custom_call_target="tpu_custom_call" | custom-call | tf_op jit(solution)/shard_map/pallas_call | solution.py:472
  119.4 1.2 %slice.3 = f32[2,3]{1,0:T(2,128)} slice(f32[8,128]{1,0:T(8,128)} %get-tuple-element.5), slice={[0:2], [0:3]} | slice | bytes 48 | tf_op jit(solution)/shard_map/slice | solution.py:485
  120.6 2.3 %copy.8 = bf16[2,512,512]{2,1,0:T(8,128)(2,1)} copy(bf16[2,512,512]{2,1,0:T(8,128)(2,1)} %get-tuple-element.8) | data formatting | bytes 2097152

commit v2 on v1

--- a/solution.py
+++ b/solution.py
@@ -151,7 +151,7 @@
         first = row_start(r)
         ids = first + lax.broadcasted_iota(jnp.int32, (quarter, 1), 0)
 
-        def body(term, carry):
+        def body(term):
             for target in range(2):
                 shift = shift_ref[term]
                 source = 2 * at.sec + target - shift
@@ -166,9 +166,9 @@
                     value = jnp.where(ids < limit, value, 0.0)
                 place = pl.multiple_of((term * 2 + target) * block + first, quarter)
                 parts[pl.ds(place, quarter), :] = value.astype(BF16)
-            return carry
-
-        lax.fori_loop(0, 4, body, 0)
+
+        for term in range(4):
+            body(term)
 
     def left_products(target, r):
         first = row_start(r)
@@ -303,17 +303,18 @@
         from_sibling(k, sides, 1)
         right_products(k, 1)
         from_sibling(k, sides, 3)
+        halo_rest(k, (2,))
         right_products(k, 3)
-        halo_rest(k, (2,))
         from_sibling(k, sides, 2)
         right_products(k, 2)
         if k == 0:
             loads[9].wait()
 
-        for r in (2, 1, 3, 0):
+        def for_sibling(r):
             sib_out[k, r] = left_products(1 - core, r).astype(BF16)
             launch(remote(sib_out.at[k, r], sib_in.at[k, r], at.sibling(), rs_sib_sem.at[k, r], k), k)
-        for r in (2, 1, 3, 0):
+
+        def for_chip(r):
             value = left_products(core, r)
             remote(sib_in.at[k, r], sib_in.at[k, r], at.sibling(), rs_sib_sem.at[k, r], k).wait_recv()
             value = value + sib_in[k, r].astype(F32)
@@ -324,6 +325,15 @@
                 launch(
                     remote(y_out.at[k, r - 1], y_in.at[k, 3 - r], at.along_y(r), rs_y_sem.at[k, 3 - r], k), k
                 )
+
+        for_sibling(2)
+        for_sibling(1)
+        for_chip(2)
+        for_sibling(3)
+        for_chip(1)
+        for_sibling(0)
+        for_chip(3)
+        for_chip(0)
 
         s = reduced(k)
         if k == 0:
@@ -379,13 +389,14 @@
         reduce_op(k + 1, sums)
 
     n = PRODUCTS
-    for h in range(2):
-        arrive(n, 0, 3, h, (["y+"] if h == 0 else []) + ["sib"])
-        arrive(n, 0, 1, h, (["y-"] if h == 1 else []) + ["sib"])
+    arrive(n, 0, 3, 0, ["y+", "sib"])
+    arrive(n, 0, 1, 0, ["sib"])
     reduce_x(n)
+    arrive(n, 0, 3, 1, ["sib"])
+    arrive(n, 0, 1, 1, ["y-", "sib"])
+    reduce_z(n)
     for h in range(2):
         arrive(n, 0, 2, h, ["sib"])
-    reduce_z(n)
     for r in range(QUARTERS):
         from_sibling(n, (0,), r)
     kept.wait()
@@ -425,7 +436,7 @@
     for i in range(PRODUCTS):
         coefs = jnp.where((row == 0) & (lane == i), alphas[i], coefs)
         coefs = jnp.where((row == 1) & (lane == i), betas[i], coefs)
-    coef_ref[...] = coefs
+    coef_ref[...] = coefs[0:2, 0:PRODUCTS]
 
     for copy in flying:
         copy.wait_send()
@@ -473,7 +484,7 @@
         functools.partial(lanczos_kernel, sec_size, op_size),
         out_shape=(
             jax.ShapeDtypeStruct(wavefunction.shape, BF16),
-            jax.ShapeDtypeStruct((8, 128), F32),
+            jax.ShapeDtypeStruct((2, PRODUCTS), F32),
         ),
         in_specs=[smem, smem, hbm, hbm, hbm],
         out_specs=(vmem, vmem),
@@ -482,7 +493,7 @@
             collective_id=0, has_side_effects=True, vmem_limit_bytes=56 * 1024 * 1024
         ),
     )(charge_shifts, sector_rows, wavefunction, left_blocks, right_blocks)
-    return vector, coefs[0:2, 0:PRODUCTS]
+    return vector, coefs
 
 
 def solution(mesh):

time: 123 us -> 116 us (0.943)
  Pallas kernels: 119 us -> 112 us
    pallas_call x1, Pallas kernels: 119 us -> 112 us  [on_device(): pl.pallas_call(functools.partial(lanczos_kernel, sec_size, op_size), out_...]
    slice x1 -> x0, local copies, waits for them, and re-layouts: 1.24 us -> none  [on_device(): return (vector, coefs[0:2, 0:PRODUCTS])]
    unnamed x1 -> x2, local copies, waits for them, and re-layouts: 2.26 us -> 3.5 us
where the time goes in v2:
time: 116 us
  Pallas kernels  112 us (97%)
  local copies, waits for them, and re-layouts  3.5 us (3%)
    pallas_call x1, Pallas kernels, on_device(): pl.pallas_call(functools.partial(lanczos_kernel, sec_size, op_size), out_...  112 us
    unnamed x2, local copies, waits for them, and re-layouts  3.5 us

profile of v2, /device:TPU:2, one launch (start us, length us, event | category | flops | bytes accessed | tf_op | source)
XLA Modules:
  0.0 115.8 jit_solution(5688056581768722775)
XLA Ops:
  0.6 111.6 %shard_map.68 = (bf16[2,512,512]{2,1,0:T(8,128)(2,1)}, f32[2,3]{1,0:T(2,128)}) custom-call(s32[4]{0:T(128)} %shift_ref.1, s32[64]{0:T(128)} %rows_ref.1, bf16[2,512,512]{2,1,0:T(8,128)(2,1)} %wave_hbm.1, bf16[4,2,512,512]{3,2,1,0:T(8,128)(2,1)} %left_hbm.1, bf16[4,512,512]{2,1,0:T(8,128)(2,1)} %right_hbm.1), custom_call_target="tpu_custom_call" | custom-call | tf_op jit(solution)/shard_map/pallas_call | solution.py:483
  112.3 2.3 %copy.9 = bf16[2,512,512]{2,1,0:T(8,128)(2,1)} copy(bf16[2,512,512]{2,1,0:T(8,128)(2,1)} %get-tuple-element.4) | data formatting | bytes 2097152
  114.5 1.2 %copy.10 = f32[2,3]{1,0:T(2,128)} copy(f32[2,3]{1,0:T(2,128)} %get-tuple-element.5) | data formatting | bytes 48

commit v3 on v2

--- a/solution.py
+++ b/solution.py
@@ -55,7 +55,7 @@
     sib_out, sib_in, y_out, y_in = take(4)
     shard_v, shard_h, shard_own = take(3)
     op_tiles, x_tiles, z_tiles = (take(PRODUCTS + 1) for _ in range(3))
-    own = [None] + take(PRODUCTS)
+    own = [None] + [take(2) for _ in range(PRODUCTS)]
     load_sem, ext_sem, sib_sem, rs_sib_sem, rs_y_sem, send_sem, op_sem, x_sem, z_sem, tile_sem = take(10)
     block, width = parts.shape[0] // 8, parts.shape[1]
     quarter = block // QUARTERS
@@ -66,6 +66,9 @@
 
     def row_start(r):
         return pl.multiple_of(((at.y + r) % QUARTERS) * quarter, quarter)
+
+    def half_start(r, h):
+        return pl.multiple_of(((at.y + r) % QUARTERS) * quarter + h * half, half)
 
     loads = []
     for r in range(QUARTERS):
@@ -124,7 +127,7 @@
     def send_piece(k, side, r, h, kind):
         src = piece(k, r, slot(k, side, True), h)
         if k > 0 and side == 0 and r == 0:
-            src = own[k].at[pl.ds(h * half, half), :]
+            src = own[k][h]
         if kind == "sib":
             to, r_to, side_to, sem = at.sibling(), r, side, sib_sem
         elif kind == "y+":
@@ -170,15 +173,13 @@
         for term in range(4):
             body(term)
 
-    def left_products(target, r):
-        first = row_start(r)
+    def left_products(target, picks):
         total = None
         for term in range(4):
+            rows = [left[term, target, pl.ds(half_start(r, h), half), :] for r, h in picks]
             place = pl.multiple_of((term * 2 + target) * block, block)
             value = jnp.dot(
-                left[term, target, pl.ds(first, quarter), :],
-                parts[pl.ds(place, block), :],
-                preferred_element_type=F32,
+                jnp.concatenate(rows, axis=0), parts[pl.ds(place, block), :], preferred_element_type=F32
             )
             total = value if total is None else total + value
         return total
@@ -234,14 +235,14 @@
         sums = jnp.sum(gathered(z_tiles, z_sem, n, at.z_size, at.z), axis=1, keepdims=True)
         return [sums[q : q + 1] / live for q in range(4)]
 
-    step_rows = 32 if quarter % 32 == 0 else 16
+    step_rows = min(32, half)
     zero_sum = jnp.zeros((8, 128), F32)
 
-    def blocks(body, carry):
-        for first in range(0, quarter, step_rows):
-            rows = pl.ds(first, step_rows)
-            ids = at.y * quarter + first + lax.broadcasted_iota(jnp.int32, (step_rows, 1), 0)
-            carry = body(rows, ids < my_rows, carry)
+    def blocks(h, body, carry):
+        for first in range(0, half, step_rows):
+            start = h * half + first
+            ids = at.y * quarter + start + lax.broadcasted_iota(jnp.int32, (step_rows, 1), 0)
+            carry = body(h, first, pl.ds(start, step_rows), ids < my_rows, carry)
         return carry
 
     halo_y = {0: lambda r, h: r in (1, 3), 1: lambda r, h: r in (1, 3) and h == 1}
@@ -254,11 +255,11 @@
         for kind in ("x+", "x-"):
             send_piece(0, 0, 2, h, kind)
 
-    def start_sum(rows, alive, carry):
+    def start_sum(h, first, rows, alive, carry):
         value = jnp.where(alive, vectors[0][0][0, rows, :].astype(F32), 0.0)
         return carry + fold(value * value)
 
-    norm = blocks(start_sum, zero_sum)
+    norm = blocks(1, start_sum, blocks(0, start_sum, zero_sum))
     reduce_op(0, [norm, zero_sum, zero_sum, zero_sum])
 
     def halo_first(k):
@@ -278,7 +279,7 @@
             for h in range(2):
                 wait_piece(k, side, r, h, sib_sem, False)
 
-    alphas, betas = [], []
+    alphas, betas, kept = [], [], []
     shift_a = scale_b = guess = None
     combos = []
     for k in range(PRODUCTS):
@@ -293,8 +294,8 @@
                 arrive(k, 0, 2, h, ["x+", "x-", "sib"])
         reduce_x(k)
         from_sibling(k, sides, 0)
-        if k > 0:
-            kept.wait()
+        for copy in kept:
+            copy.wait()
         if k == 0:
             loads[8].wait()
         right_products(k, 0)
@@ -310,30 +311,38 @@
         if k == 0:
             loads[9].wait()
 
-        def for_sibling(r):
-            sib_out[k, r] = left_products(1 - core, r).astype(BF16)
-            launch(remote(sib_out.at[k, r], sib_in.at[k, r], at.sibling(), rs_sib_sem.at[k, r], k), k)
-
-        def for_chip(r):
-            value = left_products(core, r)
-            remote(sib_in.at[k, r], sib_in.at[k, r], at.sibling(), rs_sib_sem.at[k, r], k).wait_recv()
-            value = value + sib_in[k, r].astype(F32)
-            if r == 0:
-                shard_own[...] = value
-            else:
-                y_out[k, r - 1] = value.astype(BF16)
-                launch(
-                    remote(y_out.at[k, r - 1], y_in.at[k, 3 - r], at.along_y(r), rs_y_sem.at[k, 3 - r], k), k
-                )
-
+        groups = (((2, 0), (1, 0)), ((3, 0), (0, 0)), ((2, 1), (1, 1)), ((3, 1), (0, 1)))
+
+        def for_sibling(g):
+            sib_out[k, g] = left_products(1 - core, groups[g]).astype(BF16)
+            launch(remote(sib_out.at[k, g], sib_in.at[k, g], at.sibling(), rs_sib_sem.at[k, g], k), k)
+
+        def for_chip(g):
+            value = left_products(core, groups[g])
+            remote(sib_in.at[k, g], sib_in.at[k, g], at.sibling(), rs_sib_sem.at[k, g], k).wait_recv()
+            value = value + sib_in[k, g].astype(F32)
+            for i, (r, h) in enumerate(groups[g]):
+                part = value[i * half : (i + 1) * half]
+                if r == 0:
+                    shard_own[h * half : (h + 1) * half, :] = part
+                else:
+                    y_out[k, h * 3 + r - 1] = part.astype(BF16)
+                    theirs = h * 3 + 3 - r
+                    launch(
+                        remote(
+                            y_out.at[k, h * 3 + r - 1], y_in.at[k, theirs], at.along_y(r), rs_y_sem.at[k, theirs], k
+                        ),
+                        k,
+                    )
+
+        for_sibling(0)
+        for_sibling(1)
+        for_chip(0)
         for_sibling(2)
-        for_sibling(1)
+        for_chip(1)
+        for_sibling(3)
         for_chip(2)
-        for_sibling(3)
-        for_chip(1)
-        for_sibling(0)
         for_chip(3)
-        for_chip(0)
 
         s = reduced(k)
         if k == 0:
@@ -352,16 +361,12 @@
         beta = betas[-1] if k > 0 else jnp.zeros((1, 1), F32)
         guess = next_guess
 
-        for i in range(3):
-            remote(y_in.at[k, i], y_in.at[k, i], at.sibling(), rs_y_sem.at[k, i], k).wait_recv()
-
-
-        def shard_step(rows, alive, carry):
+        def shard_step(h, first, rows, alive, carry):
             product = shard_own[rows, :]
             for i in range(3):
-                product = product + y_in[k, i, rows, :].astype(F32)
+                product = product + y_in[k, h * 3 + i, pl.ds(first, step_rows), :].astype(F32)
             product = jnp.where(alive, product, 0.0)
-            u = (vectors[0][0][0, rows, :] if k == 0 else own[k][rows, :]).astype(F32)
+            u = (vectors[0][0][0, rows, :] if k == 0 else own[k][h][pl.ds(first, step_rows), :]).astype(F32)
             if k == 0:
                 v = jnp.where(alive, u, 0.0) * inv_b
                 image = product * inv_b
@@ -374,18 +379,27 @@
             shard_v[k % 2, rows, :] = v
             shard_h[rows, :] = image
             new = new.astype(BF16)
-            own[k + 1][rows, :] = new
+            own[k + 1][h][pl.ds(first, step_rows), :] = new
             new = new.astype(F32)
             pairs = ((v, image), (new, new), (new, v), (v, v))
             return tuple(c + fold(p * q) for c, (p, q) in zip(carry, pairs))
 
-        sums = blocks(shard_step, (zero_sum,) * 4)
         kinds = ("y+", "y-", "x+", "x-", "sib") if k + 1 < PRODUCTS else ("y+", "y-", "sib")
+        sums = (zero_sum,) * 4
+        kept = []
         for h in range(2):
+            for i in range(3):
+                here = y_in.at[k, h * 3 + i]
+                remote(here, here, at.sibling(), rs_y_sem.at[k, h * 3 + i], k).wait_recv()
+            sums = blocks(h, shard_step, sums)
             for kind in kinds:
                 send_piece(k + 1, 0, 0, h, kind)
-        kept = pltpu.make_async_copy(own[k + 1], vectors[k + 1][0].at[0], load_sem.at[10 + k])
-        kept.start()
+            kept.append(
+                pltpu.make_async_copy(
+                    own[k + 1][h], vectors[k + 1][0].at[0, pl.ds(h * half, half), :], load_sem.at[10 + 2 * k + h]
+                )
+            )
+            kept[h].start()
         reduce_op(k + 1, sums)
 
     n = PRODUCTS
@@ -399,7 +413,8 @@
         arrive(n, 0, 2, h, ["sib"])
     for r in range(QUARTERS):
         from_sibling(n, (0,), r)
-    kept.wait()
+    for copy in kept:
+        copy.wait()
     s = reduced(n)
     a = s[0] - guess
     b = jnp.sqrt(s[1] - 2.0 * a * s[2] + a * a * s[3])
@@ -440,6 +455,21 @@
 
     for copy in flying:
         copy.wait_send()
+
+
+def hand_over(vector_in, coefs_in, vector_out, coefs_out, held, sems):
+    sectors, rows = held.shape[0], held.shape[1] // 2
+    places = [(s, pl.ds(i * rows, rows)) for s in range(sectors) for i in range(2)]
+    reads = [pltpu.make_async_copy(vector_in.at[p], held.at[p], sems.at[0, i]) for i, p in enumerate(places)]
+    writes = [pltpu.make_async_copy(held.at[p], vector_out.at[p], sems.at[1, i]) for i, p in enumerate(places)]
+    for read in reads:
+        read.start()
+    coefs_out[...] = coefs_in[...]
+    for read, write in zip(reads, writes):
+        read.wait()
+        write.start()
+    for write in writes:
+        write.wait()
 
 
 def on_device(sec_size, op_size, wavefunction, left_blocks, right_blocks, charge_shifts, sector_rows):
@@ -456,7 +486,7 @@
     scratch += [pltpu.VMEM((ZERO_SLOT + 1, quarter, width), BF16) for _ in range(PRODUCTS * QUARTERS)]
     scratch += [pltpu.VMEM((sectors_here, quarter, width), BF16) for _ in range(QUARTERS)]
     scratch += [pltpu.VMEM((PRODUCTS, QUARTERS, quarter, width), BF16)] * 2
-    scratch += [pltpu.VMEM((PRODUCTS, 3, quarter, width), BF16)] * 2
+    scratch += [pltpu.VMEM((PRODUCTS, 6, quarter // 2, width), BF16)] * 2
     scratch += [
         pltpu.VMEM((2, quarter, width), F32),
         pltpu.VMEM((quarter, width), F32),
@@ -464,13 +494,13 @@
     ]
     rounds = PRODUCTS + 1
     scratch += [pltpu.VMEM((count, 8, 128), F32) for count in (op_size, X_CHIPS, z_size) for _ in range(rounds)]
-    scratch += [pltpu.VMEM((quarter, width), BF16) for _ in range(PRODUCTS)]
+    scratch += [pltpu.VMEM((quarter // 2, width), BF16) for _ in range(2 * PRODUCTS)]
     scratch += [
-        dma((10 + PRODUCTS,)),
+        dma((10 + 2 * PRODUCTS,)),
         dma((rounds, QUARTERS, 3, 2)),
         dma((rounds, QUARTERS, 3, 2)),
         dma((PRODUCTS, QUARTERS)),
-        dma((PRODUCTS, 3)),
+        dma((PRODUCTS, 6)),
         dma((rounds, 64)),
         dma((rounds, op_size)),
         dma((rounds, X_CHIPS)),
@@ -493,7 +523,16 @@
             collective_id=0, has_side_effects=True, vmem_limit_bytes=56 * 1024 * 1024
         ),
     )(charge_shifts, sector_rows, wavefunction, left_blocks, right_blocks)
-    return vector, coefs
+    return pl.pallas_call(
+        hand_over,
+        out_shape=(
+            jax.ShapeDtypeStruct(wavefunction.shape, BF16),
+            jax.ShapeDtypeStruct((2, PRODUCTS), F32),
+        ),
+        in_specs=[hbm, vmem],
+        out_specs=(hbm, vmem),
+        scratch_shapes=[pltpu.VMEM(wavefunction.shape, BF16), dma((2, 4))],
+    )(vector, coefs)
 
 
 def solution(mesh):

time: 116 us -> 110 us (0.948)
  local copies, waits for them, and re-layouts: 3.5 us -> 0 us
  Pallas kernels: 112 us -> 109 us
    pallas_call x1, Pallas kernels: 112 us -> 106 us  [on_device(): pl.pallas_call(functools.partial(lanczos_kernel, sec_size, op_size), out_...]
    unnamed x2 -> x0, local copies, waits for them, and re-layouts: 3.5 us -> none
    pallas_call x0 -> x1, Pallas kernels: none -> 3.22 us  [on_device(): pl.pallas_call(hand_over, out_shape=(jax.ShapeDtypeStruct(wavefunction.sh...]
where the time goes in v3:
time: 110 us
  Pallas kernels  109 us (99%)
    pallas_call x1, Pallas kernels, on_device(): pl.pallas_call(functools.partial(lanczos_kernel, sec_size, op_size), out_...  106 us
    pallas_call x1, Pallas kernels, on_device(): pl.pallas_call(hand_over, out_shape=(jax.ShapeDtypeStruct(wavefunction.sh...  3.22 us

profile of v3, /device:TPU:2, one launch (start us, length us, event | category | flops | bytes accessed | tf_op | source)
XLA Modules:
  0.0 110.1 jit_solution(13647777505163898731)
XLA Ops:
  0.6 106.1 %shard_map.68 = (bf16[2,512,512]{2,1,0:T(8,128)(2,1)}, f32[2,3]{1,0:T(2,128)}) custom-call(s32[4]{0:T(128)} %shift_ref.1, s32[64]{0:T(128)} %rows_ref.1, bf16[2,512,512]{2,1,0:T(8,128)(2,1)} %wave_hbm.1, bf16[4,2,512,512]{3,2,1,0:T(8,128)(2,1)} %left_hbm.1, bf16[4,512,512]{2,1,0:T(8,128)(2,1)} %right_hbm.1), custom_call_target="tpu_custom_call" | custom-call | tf_op jit(solution)/shard_map/pallas_call | solution.py:513
  106.8 3.2 %shard_map.69 = (bf16[2,512,512]{2,1,0:T(8,128)(2,1)}, f32[2,3]{1,0:T(2,128)}) custom-call(bf16[2,512,512]{2,1,0:T(8,128)(2,1)} %get-tuple-element.4.vector_in, f32[2,3]{1,0:T(2,128)} %get-tuple-element.5.coefs_in), custom_call_target="tpu_custom_call" | custom-call | tf_op jit(solution)/shard_map/pallas_call | solution.py:526

commit v4 on v3

--- a/solution.py
+++ b/solution.py
@@ -55,6 +55,7 @@
     sib_out, sib_in, y_out, y_in = take(4)
     shard_v, shard_h, shard_own = take(3)
     op_tiles, x_tiles, z_tiles = (take(PRODUCTS + 1) for _ in range(3))
+    before = take(QUARTERS)
     own = [None] + [take(2) for _ in range(PRODUCTS)]
     load_sem, ext_sem, sib_sem, rs_sib_sem, rs_y_sem, send_sem, op_sem, x_sem, z_sem, tile_sem = take(10)
     block, width = parts.shape[0] // 8, parts.shape[1]
@@ -245,15 +246,11 @@
             carry = body(h, first, pl.ds(start, step_rows), ids < my_rows, carry)
         return carry
 
-    halo_y = {0: lambda r, h: r in (1, 3), 1: lambda r, h: r in (1, 3) and h == 1}
-    via_y = lambda k, r, h: halo_y[min(k, 1)](r, h)
-
-    for h in range(2):
+    via_y = lambda r, h: r in (1, 3) and h == 1
+
+    for r, h in ((0, 1), (0, 0), (1, 0), (3, 0), (2, 0), (2, 1)):
         for kind in ("x+", "x-"):
-            send_piece(0, 0, 0, h, kind)
-    for h in range(2):
-        for kind in ("x+", "x-"):
-            send_piece(0, 0, 2, h, kind)
+            send_piece(0, 0, r, h, kind)
 
     def start_sum(h, first, rows, alive, carry):
         value = jnp.where(alive, vectors[0][0][0, rows, :].astype(F32), 0.0)
@@ -263,9 +260,9 @@
     reduce_op(0, [norm, zero_sum, zero_sum, zero_sum])
 
     def halo_first(k):
-        for h in range(2):
+        for h in (1, 0) if k == 0 else (0, 1):
             for side in (1, 2):
-                kinds = ["y+", "y-"] if via_y(k, 1, h) else []
+                kinds = ["y+", "y-"] if via_y(1, h) else []
                 arrive(k, side, 0, h, kinds + ["sib"])
 
     def halo_rest(k, rs):
@@ -286,8 +283,8 @@
         sides = (1, 2) if k == 0 else (0, 1, 2)
         if k > 0:
             for h in range(2):
-                arrive(k, 0, 3, h, (["y+"] if h == 0 else []) + ([] if via_y(k, 3, h) else ["x+", "x-"]) + ["sib"])
-                arrive(k, 0, 1, h, (["y-"] if h == 1 else []) + ([] if via_y(k, 1, h) else ["x+", "x-"]) + ["sib"])
+                arrive(k, 0, 3, h, (["y+"] if h == 0 else []) + ([] if via_y(3, h) else ["x+", "x-"]) + ["sib"])
+                arrive(k, 0, 1, h, (["y-"] if h == 1 else []) + ([] if via_y(1, h) else ["x+", "x-"]) + ["sib"])
         halo_first(k)
         if k > 0:
             for h in range(2):
@@ -392,6 +389,8 @@
                 here = y_in.at[k, h * 3 + i]
                 remote(here, here, at.sibling(), rs_y_sem.at[k, h * 3 + i], k).wait_recv()
             sums = blocks(h, shard_step, sums)
+            if h == 1 and k + 1 == PRODUCTS:
+                reduce_op(k + 1, sums)
             for kind in kinds:
                 send_piece(k + 1, 0, 0, h, kind)
             kept.append(
@@ -400,7 +399,29 @@
                 )
             )
             kept[h].start()
-        reduce_op(k + 1, sums)
+        if k + 1 < PRODUCTS:
+            reduce_op(k + 1, sums)
+
+    weights = [None, None, combos[2][1]]
+    for i in (1, 0):
+        weights[i] = -weights[i + 1] * combos[i + 1][0] * combos[i][1]
+
+    def build_before():
+        for r in range(QUARTERS):
+            first = row_start(r)
+            for n, t in enumerate((core, 1 - core)):
+                limit = rows_ref[2 * at.sec + t]
+
+                def one(i, carry, r=r, n=n, limit=limit, first=first):
+                    rows = pl.ds(pl.multiple_of(i * step_rows, step_rows), step_rows)
+                    ids = first + i * step_rows + lax.broadcasted_iota(jnp.int32, (step_rows, 1), 0)
+                    value = jnp.where(ids < limit, vectors[0][r][3 * n, rows, :].astype(F32), 0.0) * weights[0]
+                    for m in (1, 2):
+                        value = value + vectors[m][r][3 * n, rows, :].astype(F32) * weights[m]
+                    before[r][n, rows, :] = value
+                    return carry
+
+                lax.fori_loop(0, quarter // step_rows, one, 0)
 
     n = PRODUCTS
     arrive(n, 0, 3, 0, ["y+", "sib"])
@@ -411,6 +432,7 @@
     reduce_z(n)
     for h in range(2):
         arrive(n, 0, 2, h, ["sib"])
+    build_before()
     for r in range(QUARTERS):
         from_sibling(n, (0,), r)
     for copy in kept:
@@ -422,28 +444,26 @@
     betas.append(b)
     combos.append((a, 1.0 / b))
 
-    weights = [None] * 4
-    factor = combos[3][1]
-    weights[3] = factor
-    for i in (2, 1, 0):
-        factor = -factor * combos[i + 1][0] * combos[i][1]
-        weights[i] = factor
-    for r in range(QUARTERS):
-        first = row_start(r)
-        for n, t in enumerate((core, 1 - core)):
-            limit = rows_ref[2 * at.sec + t]
-
-            def final(i, carry, r=r, n=n, t=t, limit=limit, first=first):
-                rows = pl.ds(pl.multiple_of(i * step_rows, step_rows), step_rows)
-                ids = first + i * step_rows + lax.broadcasted_iota(jnp.int32, (step_rows, 1), 0)
-                value = jnp.where(ids < limit, vectors[0][r][3 * n, rows, :].astype(F32), 0.0) * weights[0]
-                for m in (1, 2):
-                    value = value + vectors[m][r][3 * n, rows, :].astype(F32) * weights[m]
-                value = value + vectors[3][r][n, rows, :].astype(F32) * weights[3]
-                out_ref[t, pl.ds(pl.multiple_of(first + i * step_rows, step_rows), step_rows), :] = value.astype(BF16)
-                return carry
-
-            lax.fori_loop(0, quarter // step_rows, final, 0)
+    def each_block(body):
+        for r in range(QUARTERS):
+            first = row_start(r)
+            for n, t in enumerate((core, 1 - core)):
+
+                def one(i, carry, r=r, n=n, t=t, first=first):
+                    rows = pl.ds(pl.multiple_of(i * step_rows, step_rows), step_rows)
+                    body(r, n, t, rows, pl.multiple_of(first + i * step_rows, step_rows))
+                    return carry
+
+                lax.fori_loop(0, quarter // step_rows, one, 0)
+
+    last_scale = combos[3][1]
+    last_shift = combos[3][0]
+
+    def last(r, n, t, rows, place):
+        value = vectors[3][r][n, rows, :].astype(F32) - last_shift * before[r][n, rows, :]
+        out_ref[t, pl.ds(place, step_rows), :] = (value * last_scale).astype(BF16)
+
+    each_block(last)
 
     row = lax.broadcasted_iota(jnp.int32, (8, 128), 0)
     lane = lax.broadcasted_iota(jnp.int32, (8, 128), 1)
@@ -455,21 +475,6 @@
 
     for copy in flying:
         copy.wait_send()
-
-
-def hand_over(vector_in, coefs_in, vector_out, coefs_out, held, sems):
-    sectors, rows = held.shape[0], held.shape[1] // 2
-    places = [(s, pl.ds(i * rows, rows)) for s in range(sectors) for i in range(2)]
-    reads = [pltpu.make_async_copy(vector_in.at[p], held.at[p], sems.at[0, i]) for i, p in enumerate(places)]
-    writes = [pltpu.make_async_copy(held.at[p], vector_out.at[p], sems.at[1, i]) for i, p in enumerate(places)]
-    for read in reads:
-        read.start()
-    coefs_out[...] = coefs_in[...]
-    for read, write in zip(reads, writes):
-        read.wait()
-        write.start()
-    for write in writes:
-        write.wait()
 
 
 def on_device(sec_size, op_size, wavefunction, left_blocks, right_blocks, charge_shifts, sector_rows):
@@ -494,6 +499,7 @@
     ]
     rounds = PRODUCTS + 1
     scratch += [pltpu.VMEM((count, 8, 128), F32) for count in (op_size, X_CHIPS, z_size) for _ in range(rounds)]
+    scratch += [pltpu.VMEM((sectors_here, quarter, width), F32) for _ in range(QUARTERS)]
     scratch += [pltpu.VMEM((quarter // 2, width), BF16) for _ in range(2 * PRODUCTS)]
     scratch += [
         dma((10 + 2 * PRODUCTS,)),
@@ -513,8 +519,8 @@
     vector, coefs = pl.pallas_call(
         functools.partial(lanczos_kernel, sec_size, op_size),
         out_shape=(
-            jax.ShapeDtypeStruct(wavefunction.shape, BF16),
-            jax.ShapeDtypeStruct((2, PRODUCTS), F32),
+            pltpu.VMEM(wavefunction.shape, BF16),
+            pltpu.VMEM((2, PRODUCTS), F32),
         ),
         in_specs=[smem, smem, hbm, hbm, hbm],
         out_specs=(vmem, vmem),
@@ -523,16 +529,7 @@
             collective_id=0, has_side_effects=True, vmem_limit_bytes=56 * 1024 * 1024
         ),
     )(charge_shifts, sector_rows, wavefunction, left_blocks, right_blocks)
-    return pl.pallas_call(
-        hand_over,
-        out_shape=(
-            jax.ShapeDtypeStruct(wavefunction.shape, BF16),
-            jax.ShapeDtypeStruct((2, PRODUCTS), F32),
-        ),
-        in_specs=[hbm, vmem],
-        out_specs=(hbm, vmem),
-        scratch_shapes=[pltpu.VMEM(wavefunction.shape, BF16), dma((2, 4))],
-    )(vector, coefs)
+    return vector, coefs
 
 
 def solution(mesh):

time: 110 us -> 106 us (0.964)
  Pallas kernels: 109 us -> 103 us
  local copies, waits for them, and re-layouts: 0 us -> 1.53 us
    pallas_call x1 -> x0, Pallas kernels: 3.22 us -> none  [on_device(): pl.pallas_call(hand_over, out_shape=(jax.ShapeDtypeStruct(wavefunction.sh...]
    pallas_call x1, Pallas kernels: 106 us -> 103 us  [on_device(): pl.pallas_call(functools.partial(lanczos_kernel, sec_size, op_size), out_...]
    unnamed x0 -> x2, local copies, waits for them, and re-layouts: none -> 1.53 us
where the time goes in v4:
time: 106 us; the launch traced here: 105 us
  Pallas kernels  103 us (97%)
  local copies, waits for them, and re-layouts  1.53 us (1%)
    pallas_call x1, Pallas kernels, on_device(): pl.pallas_call(functools.partial(lanczos_kernel, sec_size, op_size), out_...  103 us

profile of v4, /device:TPU:2, one launch (start us, length us, event | category | flops | bytes accessed | tf_op | source)
XLA Modules:
  0.0 105.2 jit_solution(11870332466081502537)
XLA Ops:
  0.6 103.0 %shard_map.68 = (bf16[2,512,512]{2,1,0:T(8,128)(2,1)S(1)}, f32[2,3]{1,0:T(2,128)S(1)}) custom-call(s32[4]{0:T(128)} %shift_ref.1, s32[64]{0:T(128)} %rows_ref.1, bf16[2,512,512]{2,1,0:T(8,128)(2,1)} %wave_hbm.1, bf16[4,2,512,512]{3,2,1,0:T(8,128)(2,1)} %left_hbm.1, bf16[4,512,512]{2,1,0:T(8,128)(2,1)} %right_hbm.1), custom_call_target="tpu_custom_call" | custom-call | tf_op jit(solution)/shard_map/pallas_call | solution.py:519
  103.7 1.0 copy.9
  104.6 0.6 copy.10

commit v5 on v4

--- a/solution.py
+++ b/solution.py
@@ -89,8 +89,6 @@
     for k in range(PRODUCTS):
         for r in range(QUARTERS):
             vectors[k][r][ZERO_SLOT] = jnp.zeros((quarter, width), BF16)
-    for copy in loads[:8]:
-        copy.wait()
 
     barrier = pltpu.get_barrier_semaphore()
     partners = [(at.sec, at.op_peer(s)) for s in range(1, op_size)]
@@ -104,6 +102,8 @@
     live = jnp.full((1, 1), live_rows * width, jnp.int32).astype(F32)
     my_rows = rows_ref[2 * at.sec + core]
 
+    for copy in loads[:8]:
+        copy.wait()
     pl.semaphore_wait(barrier, len(partners))
 
     flying = []

time: 106 us -> 105 us (level)
    pallas_call x1, Pallas kernels: 103 us -> 102 us  [on_device(): pl.pallas_call(functools.partial(lanczos_kernel, sec_size, op_size), out_...]
where the time goes in v5:
time: 105 us; the launch traced here: 104 us
  Pallas kernels  102 us (97%)
  local copies, waits for them, and re-layouts  1.53 us (1%)
    pallas_call x1, Pallas kernels, on_device(): pl.pallas_call(functools.partial(lanczos_kernel, sec_size, op_size), out_...  102 us

profile of v5, /device:TPU:2, one launch (start us, length us, event | category | flops | bytes accessed | tf_op | source)
XLA Modules:
  0.0 104.1 jit_solution(6973146984852244480)
XLA Ops:
  0.6 101.9 %shard_map.68 = (bf16[2,512,512]{2,1,0:T(8,128)(2,1)S(1)}, f32[2,3]{1,0:T(2,128)S(1)}) custom-call(s32[4]{0:T(128)} %shift_ref.1, s32[64]{0:T(128)} %rows_ref.1, bf16[2,512,512]{2,1,0:T(8,128)(2,1)} %wave_hbm.1, bf16[4,2,512,512]{3,2,1,0:T(8,128)(2,1)} %left_hbm.1, bf16[4,512,512]{2,1,0:T(8,128)(2,1)} %right_hbm.1), custom_call_target="tpu_custom_call" | custom-call | tf_op jit(solution)/shard_map/pallas_call | solution.py:519
  102.6 1.0 copy.9
  103.6 0.6 copy.10
